TPU v7x, 256 devices: a whole 4x4x8 slice. The times are simulated.
256 devices in a mesh: seg: 32 (over y, x, core), fsdp: 8 (over z).
Axes of the slice: x: 4, y: 4, z: 8, core: 2. Of those that a mesh axis runs over, the one named last changes fastest.
Arguments:
- tokens: bfloat16 [8, 8192, 4096], P('fsdp', 'seg')
- w_query: bfloat16 [4096, 2048], P(('seg', 'fsdp'))
- w_key: bfloat16 [4096, 512], P(('seg', 'fsdp'))
- value_weight: bfloat16 [4096, 512], P(('seg', 'fsdp')), may hold values from -0.09375 to 0.09375
- gate_bias: float32 [16], replicated, may hold values from -2 to 2
- block_mask: int32 [8, 32, 2, 2], P('fsdp', 'seg'), may hold values from 0 to 1, as said below
- valid_len: int32 [8, 32], P('fsdp', 'seg'), may hold values from 1 to 256, as said below
Outputs:
- attended: bfloat16 [8, 8192, 2048], P('fsdp', 'seg')
Inputs may be any that keep to these rules, and one draw needn't show every extreme that they name: block_mask[b, s] is 1 on its diagonal, 0 above it, and 0 or 1 below it. `valid_len`: the first segment of every book is full.
All inputs are finite; a program needn't handle non-finite values.
Results may differ from a plain program's by a relative error of at most 0.0095.
Values may be sent and summed in bfloat16 or wider, within the bound.
A program may use at most 128 MiB of HBM per device.

v0:
```python
import jax
import jax.numpy as jnp
from jax import lax
from jax.sharding import PartitionSpec as P

HEAD_SIZE = 128
BLK = 128


def carried_in(array, axis, combine, identity):
    length, here = (lax.axis_size(axis), lax.axis_index(axis))
    everything = jax.tree.map(
        lambda part, kind: lax.all_gather(part.astype(kind), axis),
        array,
        (jnp.bfloat16, jnp.bfloat16),
    )
    start = jax.tree.map(
        lambda part, zero: jnp.broadcast_to(jnp.asarray(zero, part.dtype), part.shape),
        array,
        identity,
    )

    def lap(k, before):
        reached = k < here
        new = combine(
            before, jax.tree.map(lambda part, own: part[k].astype(own.dtype), everything, array)
        )
        return jax.tree.map(lambda a, b: jnp.where(reached, a, b), new, before)

    return lax.fori_loop(0, length, lap, start)


def sigma_plus(values):
    return jax.nn.elu(values) + 1.0


def segment_delta(keys, values, valid):
    length = keys.shape[0]
    heads_kv = keys.shape[1] // HEAD_SIZE
    live = (jnp.arange(length, dtype=jnp.int32) < valid)[:, None, None]
    sig_keys = jnp.where(
        live, sigma_plus(keys.reshape(length, heads_kv, HEAD_SIZE).astype(jnp.float32)), 0.0
    )
    delta_m = jnp.einsum(
        "jgd,jge->gde",
        sig_keys,
        values.reshape(length, heads_kv, HEAD_SIZE).astype(jnp.float32),
        precision=lax.Precision.HIGHEST,
    )
    delta_z = jnp.sum(sig_keys, axis=0)
    return (delta_m, delta_z)


def memory_before(keys, values, valid):
    delta_m, delta_z = segment_delta(keys, values, valid)

    def combine(earlier, later):
        return (earlier[0] + later[0], earlier[1] + later[1])

    identity = (jnp.zeros_like(delta_m), jnp.zeros_like(delta_z))
    memory, normalizer = carried_in((delta_m, delta_z), "seg", combine, identity)
    return (memory, normalizer)


def segment_output(queries, keys, values, gate_bias, mask_blocks, valid, memory, normalizer):
    length = queries.shape[0]
    heads_kv = memory.shape[0]
    group = queries.shape[1] // (heads_kv * HEAD_SIZE)
    nblocks = mask_blocks.shape[0]
    q_heads = queries.reshape(length, heads_kv, group, HEAD_SIZE)
    k_heads = keys.reshape(length, heads_kv, HEAD_SIZE)
    v_heads = values.reshape(length, heads_kv, HEAD_SIZE)
    scores = jnp.einsum(
        "igxd,jgd->gxij", q_heads, k_heads, preferred_element_type=jnp.float32
    ) * HEAD_SIZE ** (-0.5)
    full = jnp.broadcast_to(mask_blocks[:, None, :, None], (nblocks, BLK, nblocks, BLK)).reshape(
        length, length
    )
    pos = jnp.arange(length, dtype=jnp.int32)
    allowed = (full > 0) & (pos[None, :] <= pos[:, None]) & (pos[None, :] < valid)
    masked = jnp.where(allowed, scores, -1e30)
    top = jnp.max(masked, axis=-1, keepdims=True)
    expo = jnp.where(allowed, jnp.exp(masked - top), 0.0)
    total = jnp.maximum(jnp.sum(expo, axis=-1, keepdims=True), 1.0)
    weights = (expo / total).astype(jnp.bfloat16)
    local = jnp.einsum("gxij,jgd->igxd", weights, v_heads, preferred_element_type=jnp.float32)
    sig_q = sigma_plus(q_heads.astype(jnp.float32))
    numer = jnp.einsum("igxd,gde->igxe", sig_q, memory, precision=lax.Precision.HIGHEST)
    denom = jnp.einsum("igxd,gd->igx", sig_q, normalizer, precision=lax.Precision.HIGHEST) + 1.0
    gate = jax.nn.sigmoid(gate_bias).reshape(heads_kv, group)[None, :, :, None]
    mixed = gate * (numer / denom[..., None]) + (1.0 - gate) * local
    live = (pos < valid)[:, None, None, None]
    return jnp.where(live, mixed, 0.0).reshape(length, -1).astype(jnp.bfloat16)


def shards(tokens, w_query, w_key, value_weight, gate_bias, block_mask, valid_len):
    seg_tokens = tokens[0]
    mask_blocks = block_mask[0, 0]
    valid = valid_len[0, 0]

    def add_rows(piece):
        return jnp.dot(seg_tokens, piece, preferred_element_type=jnp.float32)

    q_sum = add_rows(lax.all_gather(w_query, ("seg", "fsdp"), axis=0, tiled=True))
    k_sum = add_rows(lax.all_gather(w_key, ("seg", "fsdp"), axis=0, tiled=True))
    v_sum = add_rows(lax.all_gather(value_weight, ("seg", "fsdp"), axis=0, tiled=True))
    keys = k_sum.astype(jnp.bfloat16)
    values = v_sum.astype(jnp.bfloat16)
    queries = q_sum.astype(jnp.bfloat16)
    memory, normalizer = memory_before(keys, values, valid)
    output = segment_output(
        queries, keys, values, gate_bias, mask_blocks, valid, memory, normalizer
    )
    return output[None]


def solution(mesh):
    in_specs = (
        P("fsdp", "seg", None),
        P(("seg", "fsdp"), None),
        P(("seg", "fsdp"), None),
        P(("seg", "fsdp"), None),
        P(),
        P("fsdp", "seg", None, None),
        P("fsdp", "seg"),
    )
    out_specs = P("fsdp", "seg", None)
    return jax.shard_map(shards, mesh=mesh, in_specs=in_specs, out_specs=out_specs, check_vma=False)
```

profile of v0, /device:TPU:1, one launch (start us, length us, event | category | flops | bytes accessed | tf_op | source)
XLA Modules:
  0.0 465.9 jit_solution(6795826982219625871)
XLA Ops:
  8.7 121.7 %all-gather.6.cloned.1.call-done = bf16[4096,512]{1,0:T(8,128)(2,1)} async-done(((bf16[16,512]{1,0:T(8,128)(2,1)}), bf16[4096,512]{1,0:T(8,128)(2,1)}) %all-gather.6.cloned.1.call-update) | async-done | bytes 4194320 | tf_op jit(solution)/shard_map/all_gather | solution.py:105
  130.4 3.6 fusion.42
  134.3 112.1 %all-gather.8.cloned.1.call-done = bf16[4096,512]{1,0:T(8,128)(2,1)} async-done(((bf16[16,512]{1,0:T(8,128)(2,1)}), bf16[4096,512]{1,0:T(8,128)(2,1)}) %all-gather.8.cloned.1.call-update) | async-done | bytes 4194320 | tf_op jit(solution)/shard_map/all_gather | solution.py:106
  246.4 3.4 fusion.28
  249.8 1.3 convolution_convert_fusion.1
  253.0 23.6 %all_gather.23 = bf16[32,4,128]{2,1,0:T(4,128)(2,1)S(1)} all-gather(bf16[1,4,128]{2,1,0:T(4,128)(2,1)S(1)} %bitcast.97), channel_id=1, replica_groups=mesh['seg'=32,'fsdp'=8] {'seg'}, dimensions={0}, use_global_device_ids=true | all-gather | bytes 33792 | tf_op jit(solution)/shard_map/all_gather | solution.py:13
  276.7 22.9 %all-gather.12.cloned.1.call-done = bf16[128,128,128]{2,1,0:T(8,128)(2,1)} async-done(((bf16[4,128,128]{2,1,0:T(8,128)(2,1)}), bf16[128,128,128]{2,1,0:T(8,128)(2,1)}) %all-gather.12.cloned.1.call-update) | async-done | bytes 4194320 | tf_op jit(solution)/shard_map/all_gather | solution.py:13
  299.6 34.6 %while.16 = (s32[]{:T(128)}, f32[4,128,128]{2,1,0:T(8,128)S(1)}, f32[4,128]{1,0:T(4,128)S(1)}, s32[]{:T(128)}, bf16[32,4,128,128]{3,2,1,0:T(8,128)(2,1)}, /*inde...) while((s32[]{:T(128)}, f32[4,128,128]{2,1,0:T(8,128)S(1)}, f32[4,128]{1,0:T(4,128)S(1)}, ...), condition=%wide.region_2.3_spmd.clone, body=%wide.region_1.2_spmd.clone.sunk | while | flops 264196 | bytes 660603 | solution.py:30
  300.7 1.0 add_select_fusion.4
  301.8 1.0 add_select_fusion.4
  302.9 1.0 add_select_fusion.4
  303.9 1.0 add_select_fusion.4
  305.0 1.0 add_select_fusion.4
  306.1 1.0 add_select_fusion.4
  307.2 1.0 add_select_fusion.4
  308.3 1.0 add_select_fusion.4
  309.4 1.0 add_select_fusion.4
  310.4 1.0 add_select_fusion.4
  311.5 1.0 add_select_fusion.4
  312.6 1.0 add_select_fusion.4
  313.7 1.0 add_select_fusion.4
  314.8 1.0 add_select_fusion.4
  315.9 1.0 add_select_fusion.4
  316.9 1.0 add_select_fusion.4
  318.0 1.0 add_select_fusion.4
  319.1 1.0 add_select_fusion.4
  320.2 1.0 add_select_fusion.4
  321.3 1.0 add_select_fusion.4
  322.4 1.0 add_select_fusion.4
  323.4 1.0 add_select_fusion.4
  324.5 1.0 add_select_fusion.4
  325.6 1.0 add_select_fusion.4
  326.7 1.0 add_select_fusion.4
  327.8 1.0 add_select_fusion.4
  328.9 1.0 add_select_fusion.4
  329.9 1.0 add_select_fusion.4
  331.0 1.0 add_select_fusion.4
  332.1 1.0 add_select_fusion.4
  333.2 1.0 add_select_fusion.4
  334.2 93.2 %all-gather.10.cloned.1.call-done = bf16[4096,2048]{1,0:T(8,128)(2,1)} async-done(((bf16[16,2048]{1,0:T(8,128)(2,1)}), bf16[4096,2048]{1,0:T(8,128)(2,1)}) %all-gather.10.cloned.1.call-update) | async-done | bytes 16777232 | tf_op jit(solution)/shard_map/all_gather | solution.py:104
  427.4 9.2 %convolution_convert_fusion = bf16[256,2048]{1,0:T(8,128)(2,1)} fusion(bf16[4096,2048]{1,0:T(8,128)(2,1)} %all-gather.10.cloned.1.call-done, bf16[1,256,4096]{2,1,0:T(8,128)(2,1)S(1)} %copy-done), kind=kOutput, calls=%fused_computation.9 | convolution fusion | flops 4295491584 | bytes 19922944 | tf_op jit(solution)/shard_map/dot_general | solution.py:102
  436.6 1.5 copy.54
  438.1 5.2 %fusion.20 = f32[4,1,256,4]{1,2,3,0:T(8,128)} fusion(f32[4,128,1,1]{1,2,3,0:T(1,128)S(1)} %bitcast.96, bf16[256,4,4,128]{0,3,2,1:T(8,128)(2,1)S(1)} %bitcast.88), kind=kOutput, calls=%fused_computation.32 | convolution fusion | flops 8916992 | bytes 1067008 | tf_op jit(solution)/shard_map/igxd,gd->igx/dot_general | solution.py:89
  443.3 2.2 copy.57
  445.5 4.7 %fusion.69 = (f32[4,4,256]{2,1,0:T(4,128)S(1)}, f32[4,4,256,256]{2,3,1,0:T(8,128)}) fusion(pred[256,256]{0,1:T(8,128)(4,1)S(1)} %copy.35, bf16[256,4,4,128]{0,3,2,1:T(8,128)(2,1)S(1)} %bitcast.89, bf16[256,4,128,1]{2,1,0,3:T(4,128)(2,1)} %bitcast.92), kind=kOutput, calls=%fused_computation.76 | convolution fusion | flops 273678592 | bytes 5586944 | tf_op jit(solution)/shard_map/sub | solution.py:83
  450.2 2.8 fusion.14
  453.1 4.1 fusion.5
  457.1 2.3 copy.40
  (64 shorter events, 5.1 us)
Async XLA Ops:
  6.5 123.8 %copy-start = (bf16[1,256,4096]{2,1,0:T(8,128)(2,1)S(1)}, bf16[1,256,4096]{2,1,0:T(8,128)(2,1)}, u32[]{:S(2)}) copy-start(bf16[1,256,4096]{2,1,0:T(8,128)(2,1)} %param.9) | copy-start | bytes 6291460
  6.5 123.8 %all-gather.6.cloned.1.call-start = ((), (), s32[]{:S(2)}) async-start(), calls=%async_computation | async-start | bytes 4210688 | tf_op jit(solution)/shard_map/all_gather | solution.py:105
  7.3 239.1 %all-gather.8.cloned.1.call-start = ((), (), s32[]{:S(2)}) async-start(), calls=%async_computation.1 | async-start | bytes 4210688 | tf_op jit(solution)/shard_map/all_gather | solution.py:106
  8.0 291.6 %all-gather.12.cloned.1.call-start = ((), (), s32[]{:S(2)}) async-start(), calls=%async_computation.3 | async-start | bytes 4325376 | tf_op jit(solution)/shard_map/all_gather | solution.py:13
  134.1 115.7 %copy-start.1 = (bf16[256,4,128]{2,1,0:T(4,128)(2,1)}, bf16[256,4,128]{2,1,0:T(4,128)(2,1)S(1)}, u32[]{:S(2)}) copy-start(bf16[256,4,128]{2,1,0:T(4,128)(2,1)S(1)} %reshape.73) | copy-start | bytes 786436
  134.3 117.5 %copy-start.3 = (f32[16]{0:T(128)S(1)}, f32[16]{0:T(128)}, u32[]{:S(2)}) copy-start(f32[16]{0:T(128)} %param.13) | copy-start | bytes 196
  134.3 117.6 %copy-start.2 = (s32[1,1,2,2]{3,2,1,0:T(2,128)S(1)}, s32[1,1,2,2]{3,2,1,0:T(2,128)}, u32[]{:S(2)}) copy-start(s32[1,1,2,2]{3,2,1,0:T(2,128)} %param.14) | copy-start | bytes 52
  251.1 176.3 %all-gather.10.cloned.1.call-start = ((), (), s32[]{:S(2)}) async-start(), calls=%async_computation.2 | async-start | bytes 16842752 | tf_op jit(solution)/shard_map/all_gather | solution.py:104
Sparse Core Ops, SparseCore 0:
  11.0 119.3 all-gather.5
  134.0 112.3 all-gather.7
  251.3 48.3 all-gather.11
  303.1 124.3 all-gather.9
where the time goes:
time: 467 us; the launch traced here: 466 us
  waiting for transfers between devices  352 us (75%)
  matrix products  34.3 us (7%)
  other arithmetic  33.9 us (7%)
  blocking collectives  23.6 us (5%)
  between operations  13.9 us (3%)
  local copies, waits for them, and re-layouts  7.38 us (2%)
    all_gather x1, waiting for transfers between devices, shards(): k_sum = add_rows(lax.all_gather(w_key, ('seg', 'fsdp'), axis=0, tiled=True))  122 us
    all_gather x1, waiting for transfers between devices, shards(): lax.all_gather(value_weight, ('seg', 'fsdp'), axis=0, tiled=True)  112 us
    all_gather x1, waiting for transfers between devices, shards(): lax.all_gather(w_query, ('seg', 'fsdp'), axis=0, tiled=True)  93.2 us
    select_n x64, other arithmetic, lap(): return jax.tree.map(lambda a, b: jnp.where(reached, a, b), new, before)  33.8 us
    all_gather x1, blocking collectives, carried_in(): lax.all_gather(part.astype(kind), axis)  23.6 us
    all_gather x1, waiting for transfers between devices, carried_in(): lax.all_gather(part.astype(kind), axis)  22.9 us
    dot_general x3, matrix products, add_rows(): return jnp.dot(seg_tokens, piece, preferred_element_type=jnp.float32)  16.3 us
  transfers between devices with their start and end apart: 4, of which 4 were waited for; matrix products, arithmetic and copies ran while one was open for 8% of the time, Pallas kernels for 0%

commit v1 on v0

--- a/solution.py
+++ b/solution.py
@@ -103,7 +103,14 @@
 
     q_sum = add_rows(lax.all_gather(w_query, ("seg", "fsdp"), axis=0, tiled=True))
     k_sum = add_rows(lax.all_gather(w_key, ("seg", "fsdp"), axis=0, tiled=True))
-    v_sum = add_rows(lax.all_gather(value_weight, ("seg", "fsdp"), axis=0, tiled=True))
+    v_sum = add_rows(
+        jnp.concatenate(
+            lax.all_to_all(
+                jnp.stack([value_weight] * lax.axis_size(("seg", "fsdp"))), ("seg", "fsdp"), 0, 0
+            ),
+            axis=0,
+        )
+    )
     keys = k_sum.astype(jnp.bfloat16)
     values = v_sum.astype(jnp.bfloat16)
     queries = q_sum.astype(jnp.bfloat16)

time: 467 us -> 369 us (0.79)
  waiting for transfers between devices: 352 us -> 233 us
  starting transfers between devices: 0.12 us -> 16.7 us
    all_gather x1 -> x0, waiting for transfers between devices: 112 us -> none  [shards(): lax.all_gather(value_weight, ('seg', 'fsdp'), axis=0, tiled=True)]
    all_to_all x0 -> x1, starting transfers between devices: none -> 16.7 us  [shards(): lax.all_to_all(jnp.stack([value_weight] * lax.axis_size(('seg', 'fsdp')))...]
    all_gather x1, waiting for transfers between devices: 122 us -> 115 us  [shards(): k_sum = add_rows(lax.all_gather(w_key, ('seg', 'fsdp'), axis=0, tiled=True))]
  transfers between devices with their start and end apart: 4 -> 4, of which waited for: 4 -> 3; matrix products, arithmetic and copies ran while one was open for 8% -> 11% of each run, Pallas kernels for 0% -> 0%
where the time goes in v1:
time: 369 us; the launch traced here: 368 us
  waiting for transfers between devices  233 us (63%)
  matrix products  34.3 us (9%)
  other arithmetic  33.9 us (9%)
  blocking collectives  24.8 us (7%)
  starting transfers between devices  16.7 us (5%)
  between operations  13.9 us (4%)
  local copies, waits for them, and re-layouts  10.6 us (3%)
    all_gather x1, waiting for transfers between devices, shards(): k_sum = add_rows(lax.all_gather(w_key, ('seg', 'fsdp'), axis=0, tiled=True))  115 us
    all_gather x1, waiting for transfers between devices, shards(): lax.all_gather(w_query, ('seg', 'fsdp'), axis=0, tiled=True)  93.3 us
    select_n x64, other arithmetic, lap(): return jax.tree.map(lambda a, b: jnp.where(reached, a, b), new, before)  33.8 us
    all_gather x1, blocking collectives, carried_in(): lax.all_gather(part.astype(kind), axis)  24.8 us
    all_gather x1, waiting for transfers between devices, carried_in(): lax.all_gather(part.astype(kind), axis)  22.7 us
    all_to_all x1, starting transfers between devices, shards(): lax.all_to_all(jnp.stack([value_weight] * lax.axis_size(('seg', 'fsdp')))...  16.7 us
    dot_general x3, matrix products, add_rows(): return jnp.dot(seg_tokens, piece, preferred_element_type=jnp.float32)  16.3 us
  transfers between devices with their start and end apart: 4, of which 3 were waited for; matrix products, arithmetic and copies ran while one was open for 11% of the time, Pallas kernels for 0%

profile of v1, /device:TPU:1, one launch (start us, length us, event | category | flops | bytes accessed | tf_op | source)
XLA Modules:
  0.0 367.9 jit_solution(13849976453319017268)
XLA Ops:
  7.3 3.2 stack.2
  10.5 16.7 %all-to-all-start = ((bf16[256,16,512]{2,1,0:T(8,128)(2,1)}), bf16[256,16,512]{2,1,0:T(8,128)(2,1)}, u32[]{:S(2)}, u32[]{:S(2)}) async-start(bf16[256,16,512]{2,1,0:T(8,128)(2,1)} %stack.2), calls=%async_computation | async-start | bytes 8388608 | tf_op jit(solution)/shard_map/all_to_all | solution.py:108
  27.9 115.4 %all-gather.5.cloned.1.call-done = bf16[4096,512]{1,0:T(8,128)(2,1)} async-done(((bf16[16,512]{1,0:T(8,128)(2,1)}), bf16[4096,512]{1,0:T(8,128)(2,1)}) %all-gather.5.cloned.1.call-update) | async-done | bytes 4194320 | tf_op jit(solution)/shard_map/all_gather | solution.py:105
  143.2 3.6 fusion.42
  147.2 3.4 fusion.28
  150.6 1.3 convolution_convert_fusion.1
  154.0 24.8 %all_gather.19 = bf16[32,4,128]{2,1,0:T(4,128)(2,1)S(1)} all-gather(bf16[1,4,128]{2,1,0:T(4,128)(2,1)S(1)} %bitcast.98), channel_id=1, replica_groups=mesh['seg'=32,'fsdp'=8] {'seg'}, dimensions={0}, use_global_device_ids=true | all-gather | bytes 33792 | tf_op jit(solution)/shard_map/all_gather | solution.py:13
  178.8 22.7 %all-gather.9.cloned.1.call-done = bf16[128,128,128]{2,1,0:T(8,128)(2,1)} async-done(((bf16[4,128,128]{2,1,0:T(8,128)(2,1)}), bf16[128,128,128]{2,1,0:T(8,128)(2,1)}) %all-gather.9.cloned.1.call-update) | async-done | bytes 4194320 | tf_op jit(solution)/shard_map/all_gather | solution.py:13
  201.5 34.6 %while.16 = (s32[]{:T(128)}, f32[4,128,128]{2,1,0:T(8,128)S(1)}, f32[4,128]{1,0:T(4,128)S(1)}, s32[]{:T(128)}, bf16[32,4,128,128]{3,2,1,0:T(8,128)(2,1)}, /*inde...) while((s32[]{:T(128)}, f32[4,128,128]{2,1,0:T(8,128)S(1)}, f32[4,128]{1,0:T(4,128)S(1)}, ...), condition=%wide.region_2.3_spmd.clone, body=%wide.region_1.2_spmd.clone.sunk | while | flops 264196 | bytes 660603 | solution.py:30
  202.6 1.0 add_select_fusion.4
  203.7 1.0 add_select_fusion.4
  204.8 1.0 add_select_fusion.4
  205.8 1.0 add_select_fusion.4
  206.9 1.0 add_select_fusion.4
  208.0 1.0 add_select_fusion.4
  209.1 1.0 add_select_fusion.4
  210.2 1.0 add_select_fusion.4
  211.3 1.0 add_select_fusion.4
  212.3 1.0 add_select_fusion.4
  213.4 1.0 add_select_fusion.4
  214.5 1.0 add_select_fusion.4
  215.6 1.0 add_select_fusion.4
  216.7 1.0 add_select_fusion.4
  217.8 1.0 add_select_fusion.4
  218.8 1.0 add_select_fusion.4
  219.9 1.0 add_select_fusion.4
  221.0 1.0 add_select_fusion.4
  222.1 1.0 add_select_fusion.4
  223.2 1.0 add_select_fusion.4
  224.3 1.0 add_select_fusion.4
  225.3 1.0 add_select_fusion.4
  226.4 1.0 add_select_fusion.4
  227.5 1.0 add_select_fusion.4
  228.6 1.0 add_select_fusion.4
  229.7 1.0 add_select_fusion.4
  230.8 1.0 add_select_fusion.4
  231.8 1.0 add_select_fusion.4
  232.9 1.0 add_select_fusion.4
  234.0 1.0 add_select_fusion.4
  236.1 93.3 %all-gather.7.cloned.1.call-done = bf16[4096,2048]{1,0:T(8,128)(2,1)} async-done(((bf16[16,2048]{1,0:T(8,128)(2,1)}), bf16[4096,2048]{1,0:T(8,128)(2,1)}) %all-gather.7.cloned.1.call-update) | async-done | bytes 16777232 | tf_op jit(solution)/shard_map/all_gather | solution.py:104
  329.5 9.2 %convolution_convert_fusion = bf16[256,2048]{1,0:T(8,128)(2,1)} fusion(bf16[4096,2048]{1,0:T(8,128)(2,1)} %all-gather.7.cloned.1.call-done, bf16[1,256,4096]{2,1,0:T(8,128)(2,1)S(1)} %copy-done), kind=kOutput, calls=%fused_computation.9 | convolution fusion | flops 4295491584 | bytes 19922944 | tf_op jit(solution)/shard_map/dot_general | solution.py:102
  338.7 1.5 copy.54
  340.1 4.7 %fusion.69 = (f32[4,4,256]{2,1,0:T(4,128)S(1)}, f32[4,4,256,256]{2,3,1,0:T(8,128)}) fusion(pred[256,256]{0,1:T(8,128)(4,1)S(1)} %copy.35, bf16[256,4,4,128]{0,3,2,1:T(8,128)(2,1)S(1)} %bitcast.89, bf16[256,4,128,1]{2,1,0,3:T(4,128)(2,1)} %bitcast.93), kind=kOutput, calls=%fused_computation.76 | convolution fusion | flops 273678592 | bytes 5586944 | tf_op jit(solution)/shard_map/sub | solution.py:83
  344.8 5.2 %fusion.20 = f32[4,1,256,4]{1,2,3,0:T(8,128)} fusion(f32[4,128,1,1]{1,2,3,0:T(1,128)S(1)} %bitcast.97, bf16[256,4,4,128]{0,3,2,1:T(8,128)(2,1)S(1)} %bitcast.90), kind=kOutput, calls=%fused_computation.32 | convolution fusion | flops 8916992 | bytes 1067008 | tf_op jit(solution)/shard_map/igxd,gd->igx/dot_general | solution.py:89
  350.0 2.2 copy.57
  352.2 2.8 fusion.14
  355.1 4.1 %fusion.5 = bf16[256,4,4,128]{0,3,2,1:T(8,128)(2,1)} fusion(f32[4,128,4,256]{3,1,2,0:T(8,128)S(1)} %fusion.14, bf16[256,4,4,128]{0,3,2,1:T(8,128)(2,1)S(1)} %bitcast.91, f32[4,4]{1,0:T(4,128)S(1)} %broadcast_subtract_fusion, f32[256,4,4]{0,2,1:T(4,128)S(1)} %bitcast_bitcast_fusion, f32[4,4]{1,0:T(4,128)S(1)} %mul.30, ...), kind=kOutput, calls=%fused_computation.14 | convolution fusion | flops 811073536 | bytes 4473216 | tf_op jit(solution)/shard_map/igxd,gde->igxe/dot_general | solution.py:88
  359.1 2.3 copy.40
  (64 shorter events, 5.6 us)
Async XLA Ops:
  6.5 136.7 %copy-start = (bf16[1,256,4096]{2,1,0:T(8,128)(2,1)S(1)}, bf16[1,256,4096]{2,1,0:T(8,128)(2,1)}, u32[]{:S(2)}) copy-start(bf16[1,256,4096]{2,1,0:T(8,128)(2,1)} %param.9) | copy-start | bytes 6291460
  6.5 136.7 %all-gather.5.cloned.1.call-start = ((), (), s32[]{:S(2)}) async-start(), calls=%async_computation.1 | async-start | bytes 4210688 | tf_op jit(solution)/shard_map/all_gather | solution.py:105
  10.5 136.6 %all-to-all-start = ((bf16[256,16,512]{2,1,0:T(8,128)(2,1)}), bf16[256,16,512]{2,1,0:T(8,128)(2,1)}, u32[]{:S(2)}, u32[]{:S(2)}) async-start(bf16[256,16,512]{2,1,0:T(8,128)(2,1)} %stack.2), calls=%async_computation | async-start | bytes 8388608 | tf_op jit(solution)/shard_map/all_to_all | solution.py:108
  27.1 174.4 %all-gather.9.cloned.1.call-start = ((), (), s32[]{:S(2)}) async-start(), calls=%async_computation.3 | async-start | bytes 4325376 | tf_op jit(solution)/shard_map/all_gather | solution.py:13
  146.9 3.7 copy-start.1
  147.1 5.5 %copy-start.3 = (f32[16]{0:T(128)S(1)}, f32[16]{0:T(128)}, u32[]{:S(2)}) copy-start(f32[16]{0:T(128)} %param.13) | copy-start | bytes 196
  147.2 5.6 %copy-start.2 = (s32[1,1,2,2]{3,2,1,0:T(2,128)S(1)}, s32[1,1,2,2]{3,2,1,0:T(2,128)}, u32[]{:S(2)}) copy-start(s32[1,1,2,2]{3,2,1,0:T(2,128)} %param.14) | copy-start | bytes 52
  151.9 177.6 %all-gather.7.cloned.1.call-start = ((), (), s32[]{:S(2)}) async-start(), calls=%async_computation.2 | async-start | bytes 16842752 | tf_op jit(solution)/shard_map/all_gather | solution.py:104
Sparse Core Ops, SparseCore 0:
  11.0 132.2 all-gather.4
  152.0 49.4 all-gather.8
  205.1 124.3 all-gather.6
